TPU v7x, 128 devices: a whole 4x4x4 slice. The times are simulated.
128 devices in a mesh: group: 4 (over z_lo, core), dp: 2 (over z_hi), tensor: 16 (over x, y).
Axes of the slice: x: 4, y: 4, z: 4 (z_hi: 2, z_lo: 2; z = z_hi * 2 + z_lo), core: 2. Of those that a mesh axis runs over, the one named last changes fastest.
Arguments:
- tokens: bfloat16 [2048, 8, 2048], P('tensor', ('group', 'dp')), may hold values from -6 to 6
- cotangent: bfloat16 [2048, 8, 2048], P('tensor', ('group', 'dp')), may hold values from -6 to 6
- lengths: int32 [8], replicated, may hold values from 1 to 2048, 9830 in all
- ln1_gain: float32 [2048], replicated, may hold values from 0.25 to 1.75
- ln1_bias: float32 [2048], replicated, may hold values from -1.75 to 1.75
- w_qkv: bfloat16 [2048, 3, 16, 128], P(None, None, 'tensor'), may hold values from -0.125 to 0.125
- b_qv: float32 [2, 2048], P(None, 'tensor'), may hold values from -1.75 to 1.75
- w_o: bfloat16 [16, 128, 2048], P('tensor'), may hold values from -0.75 to 0.75
- b_o: float32 [2048], replicated, may hold values from -1.75 to 1.75
- ln2_gain: float32 [2048], replicated, may hold values from 0.25 to 1.75
- ln2_bias: float32 [2048], replicated, may hold values from -1.75 to 1.75
- w_in: bfloat16 [2048, 8192], P(None, 'tensor'), may hold values from -0.125 to 0.125
- b_in: float32 [8192], P('tensor'), may hold values from -1.75 to 1.75
- w_out: bfloat16 [8192, 2048], P('tensor'), may hold values from -0.0625 to 0.0625
- b_out: float32 [2048], replicated, may hold values from -1.75 to 1.75
Outputs:
- output: bfloat16 [2048, 8, 2048], P('tensor', ('group', 'dp'))
- input_grad: bfloat16 [2048, 8, 2048], P('tensor', ('group', 'dp'))
- d_ln1_gain: float32 [2048], P(('group', 'dp', 'tensor'))
- d_ln1_bias: float32 [2048], P(('group', 'dp', 'tensor'))
- d_w_qkv: float32 [2048, 3, 16, 128], P(('group', 'dp'), None, 'tensor')
- d_b_qv: float32 [2, 2048], P(None, ('group', 'dp', 'tensor'))
- d_w_o: float32 [16, 128, 2048], P('tensor', None, ('group', 'dp'))
- d_b_o: float32 [2048], P(('group', 'dp', 'tensor'))
- d_ln2_gain: float32 [2048], P(('group', 'dp', 'tensor'))
- d_ln2_bias: float32 [2048], P(('group', 'dp', 'tensor'))
- d_w_in: float32 [2048, 8192], P(('group', 'dp'), 'tensor')
- d_b_in: float32 [8192], P(('group', 'dp', 'tensor'))
- d_w_out: float32 [8192, 2048], P('tensor', ('group', 'dp'))
- d_b_out: float32 [2048], P(('group', 'dp', 'tensor'))
Inputs may be any that keep to these rules, and one draw needn't show every extreme that they name: The true lengths of the 8 sequences sum to 9830.
All inputs are finite; a program needn't handle non-finite values.
Results may differ from a plain program's by a relative error of at most 0.02.
Values may be sent and summed in bfloat16 or wider, within the bound.
No kernel may reach another device: no remote copies, remote signals or barrier semaphores. Data moves between devices by JAX's collectives and lax.ppermute only.
A program may use at most 192 MiB of HBM per device.

v0:
```python
from functools import partial
import math
import jax
import jax.numpy as jnp
from jax import lax
from jax.sharding import PartitionSpec as P

EPS = 1e-05
NEGATIVE = -1e30


def layer_norm(value, gain, shift):
    mean = jnp.mean(value, axis=-1, keepdims=True)
    centred = value - mean
    spread = jnp.mean(centred * centred, axis=-1, keepdims=True)
    return centred * lax.rsqrt(spread + EPS) * gain + shift


def gelu_tanh(value):
    return jax.nn.gelu(value, approximate=True)


def block_scores(rows_query, key_rows, first, length, score_scale):
    count = rows_query.shape[0]
    key_pos = jnp.arange(key_rows.shape[0], dtype=jnp.int32)
    query_pos = first + jnp.arange(count, dtype=jnp.int32)
    valid = (key_pos[None, :] <= query_pos[:, None]) & (key_pos[None, :] < length)
    scores = (
        lax.dot_general(
            rows_query, key_rows, (((1,), (1,)), ((), ())), preferred_element_type=jnp.float32
        )
        * score_scale
    )
    return (jnp.where(valid, scores, NEGATIVE), valid)


def attend_forward(item, block_rows, score_scale):
    query, key_rows, value_rows, length = item
    outputs = []
    log_parts = []
    for first in range(0, query.shape[0], block_rows):
        rows_query = query[first : first + block_rows]
        scores, valid = block_scores(rows_query, key_rows, first, length, score_scale)
        peak = jnp.max(scores, axis=-1, keepdims=True)
        expo = jnp.exp(scores - peak)
        weight_sum = jnp.sum(expo, axis=-1, keepdims=True)
        probs = (expo / weight_sum).astype(jnp.bfloat16)
        outputs.append(
            jnp.dot(probs, value_rows, preferred_element_type=jnp.float32).astype(jnp.bfloat16)
        )
        log_parts.append((peak + jnp.log(weight_sum))[:, 0])
    return (jnp.concatenate(outputs, 0), jnp.concatenate(log_parts, 0))


def attend_backward(item, block_rows, score_scale):
    query, key_rows, value_rows, length, grad_out, log_sums = item
    key_grad = jnp.zeros(key_rows.shape, jnp.float32)
    value_grad = jnp.zeros(value_rows.shape, jnp.float32)
    query_parts = []
    for first in range(0, query.shape[0], block_rows):
        rows_query = query[first : first + block_rows]
        scores, valid = block_scores(rows_query, key_rows, first, length, score_scale)
        probs = jnp.where(valid, jnp.exp(scores - log_sums[first : first + block_rows, None]), 0.0)
        grad_rows = grad_out[first : first + block_rows]
        probs_grad = lax.dot_general(
            grad_rows, value_rows, (((1,), (1,)), ((), ())), preferred_element_type=jnp.float32
        )
        inner = jnp.sum(probs * probs_grad, axis=-1, keepdims=True)
        score_grad = (probs * (probs_grad - inner)).astype(jnp.bfloat16)
        query_parts.append(
            jnp.dot(score_grad, key_rows, preferred_element_type=jnp.float32) * score_scale
        )
        key_grad = (
            key_grad
            + lax.dot_general(
                score_grad, rows_query, (((0,), (0,)), ((), ())), preferred_element_type=jnp.float32
            )
            * score_scale
        )
        value_grad = value_grad + lax.dot_general(
            probs.astype(jnp.bfloat16),
            grad_rows,
            (((0,), (0,)), ((), ())),
            preferred_element_type=jnp.float32,
        )
    return (
        jnp.concatenate(query_parts, 0).astype(jnp.bfloat16),
        key_grad.astype(jnp.bfloat16),
        value_grad.astype(jnp.bfloat16),
    )


def shards(
    tokens,
    cotangent,
    lengths,
    ln1_gain,
    ln1_bias,
    w_qkv,
    b_qv,
    w_o,
    b_o,
    ln2_gain,
    ln2_bias,
    w_in,
    b_in,
    w_out,
    b_out,
):
    row_count, seq_count, model_width = tokens.shape
    tensor_count = lax.axis_size("tensor")
    tensor_rank = lax.axis_index("tensor")
    seq_total = row_count * tensor_count
    local_heads = w_qkv.shape[2]
    head_size = w_qkv.shape[3]
    local_width = local_heads * head_size
    hidden = w_in.shape[1]
    block_rows = min(512, seq_total)
    score_scale = 1.0 / math.sqrt(head_size)
    group_count = lax.axis_size("group")
    group_rank = lax.axis_index("group")
    member = group_rank * lax.axis_size("dp") + lax.axis_index("dp")
    seq_lengths = lax.dynamic_slice_in_dim(lengths, member * seq_count, seq_count, 0)
    group_totals = jnp.sum(lengths.reshape(group_count, -1), axis=1).astype(jnp.float32)
    factor = (
        group_count
        * lax.dynamic_index_in_dim(group_totals, group_rank, 0, keepdims=False)
        / jnp.sum(group_totals)
    )
    inputs = tokens.astype(jnp.float32)
    normed_low = layer_norm(inputs, ln1_gain, ln1_bias).astype(jnp.bfloat16)
    normed_full = lax.all_gather(normed_low, "tensor", axis=0, tiled=True)
    joint_weight = w_qkv.reshape(model_width, 3 * local_width)
    projected = jnp.dot(
        normed_full.reshape(seq_total * seq_count, model_width),
        joint_weight,
        preferred_element_type=jnp.float32,
    )
    projected = projected.reshape(seq_total, seq_count, 3, local_width)
    query = (projected[:, :, 0] + b_qv[0]).astype(jnp.bfloat16)
    keys = projected[:, :, 1].astype(jnp.bfloat16)
    values = (projected[:, :, 2] + b_qv[1]).astype(jnp.bfloat16)

    def per_item(array):
        shaped = array.reshape(seq_total, seq_count, local_heads, head_size)
        return jnp.transpose(shaped, (1, 2, 0, 3)).reshape(
            seq_count * local_heads, seq_total, head_size
        )

    def per_row(array):
        shaped = array.reshape(seq_count, local_heads, seq_total, head_size)
        return jnp.transpose(shaped, (2, 0, 1, 3)).reshape(seq_total, seq_count, local_width)

    query_items = per_item(query)
    key_items = per_item(keys)
    value_items = per_item(values)
    item_lengths = jnp.repeat(seq_lengths, local_heads)
    heads_out, log_sums = lax.map(
        partial(attend_forward, block_rows=block_rows, score_scale=score_scale),
        (query_items, key_items, value_items, item_lengths),
    )
    attended = per_row(heads_out)
    out_weight = w_o.reshape(local_width, model_width)
    positions = tensor_rank * row_count + jnp.arange(row_count, dtype=jnp.int32)
    live = positions[:, None] < seq_lengths[None, :]
    upstream = jnp.where(live[:, :, None], cotangent, jnp.zeros_like(cotangent))
    upstream_full = lax.all_gather(upstream, "tensor", axis=0, tiled=True)
    attention_part = jnp.einsum(
        "rse,ed->rsd", attended, out_weight, preferred_element_type=jnp.float32
    ).astype(jnp.bfloat16)
    attention_part, upstream_full = lax.optimization_barrier((attention_part, upstream_full))
    attention = (
        lax.psum_scatter(attention_part, "tensor", scatter_dimension=0, tiled=True).astype(
            jnp.float32
        )
        + b_o
    )
    middle = inputs + attention
    second_low = layer_norm(middle, ln2_gain, ln2_bias).astype(jnp.bfloat16)
    second_full = lax.all_gather(second_low, "tensor", axis=0, tiled=True)
    pre_act = (
        jnp.dot(
            second_full.reshape(seq_total * seq_count, model_width),
            w_in,
            preferred_element_type=jnp.float32,
        )
        + b_in
    )
    activated = gelu_tanh(pre_act).astype(jnp.bfloat16).reshape(seq_total, seq_count, hidden)
    feed_part = jnp.einsum(
        "rsf,fd->rsd", activated, w_out, preferred_element_type=jnp.float32
    ).astype(jnp.bfloat16)
    piece = upstream_full
    weight_grad = jnp.einsum("rsf,rsd->fd", activated, piece, preferred_element_type=jnp.float32)
    part = jnp.einsum("rsd,fd->rsf", piece, w_out, preferred_element_type=jnp.float32)
    act_grad = part
    grad_w_out = weight_grad
    gelu_back = jax.vjp(gelu_tanh, pre_act)[1]
    pre_low = gelu_back(act_grad.reshape(seq_total * seq_count, hidden))[0].astype(jnp.bfloat16)
    grad_b_in = jnp.sum(pre_low, axis=0, dtype=jnp.float32)
    grad_w_in = jnp.einsum(
        "rd,rf->df",
        second_full.reshape(seq_total * seq_count, model_width),
        pre_low,
        preferred_element_type=jnp.float32,
    )
    pre_rows = pre_low.reshape(seq_total, seq_count, hidden)
    piece = pre_rows
    second_grad = lax.psum_scatter(
        jnp.einsum("rsf,df->rsd", piece, w_in, preferred_element_type=jnp.float32).astype(
            jnp.bfloat16
        ),
        "tensor",
        scatter_dimension=0,
        tiled=True,
    ).astype(jnp.float32)
    norm_two_back = jax.vjp(layer_norm, middle, ln2_gain, ln2_bias)[1]
    middle_part, grad_ln2_gain, grad_ln2_bias = norm_two_back(second_grad)
    middle_grad = upstream.astype(jnp.float32) + middle_part
    branch_low = middle_grad.astype(jnp.bfloat16)
    grad_b_o = jnp.sum(branch_low, axis=(0, 1), dtype=jnp.float32)
    grad_b_out = jnp.sum(upstream, axis=(0, 1), dtype=jnp.float32)
    piece = lax.all_gather(branch_low, "tensor", axis=0, tiled=True)
    feed_part, piece = lax.optimization_barrier((feed_part, piece))
    feed = (
        lax.psum_scatter(feed_part, "tensor", scatter_dimension=0, tiled=True).astype(jnp.float32)
        + b_out
    )
    output = (middle + feed).astype(jnp.bfloat16)
    weight_grad = jnp.einsum("rse,rsd->ed", attended, piece, preferred_element_type=jnp.float32)
    part = jnp.einsum("rsd,ed->rse", piece, out_weight, preferred_element_type=jnp.float32)
    head_items = per_item(part.astype(jnp.bfloat16))
    grads_query, grads_keys, grads_values = lax.map(
        partial(attend_backward, block_rows=block_rows, score_scale=score_scale),
        (query_items, key_items, value_items, item_lengths, head_items, log_sums),
    )
    joint_grad = jnp.stack(
        (per_row(grads_query), per_row(grads_keys), per_row(grads_values)), axis=2
    )
    grad_b_qv = jnp.sum(joint_grad[:, :, 0::2], axis=(0, 1), dtype=jnp.float32)
    joint_rows = joint_grad.reshape(seq_total, seq_count, 3 * local_width)
    grad_w_qkv = jnp.einsum(
        "rd,rc->dc",
        normed_full.reshape(seq_total * seq_count, model_width),
        joint_rows.reshape(seq_total * seq_count, 3 * local_width),
        preferred_element_type=jnp.float32,
    )
    piece = joint_rows
    normed_grad = lax.psum_scatter(
        jnp.einsum("rsc,dc->rsd", piece, joint_weight, preferred_element_type=jnp.float32).astype(
            jnp.bfloat16
        ),
        "tensor",
        scatter_dimension=0,
        tiled=True,
    ).astype(jnp.float32)
    norm_one_back = jax.vjp(layer_norm, inputs, ln1_gain, ln1_bias)[1]
    input_part, grad_ln1_gain, grad_ln1_bias = norm_one_back(normed_grad)
    input_grad = (middle_grad + input_part).astype(jnp.bfloat16)
    summed = (
        halving_sum(grad_w_qkv.reshape(model_width, 3, local_heads, head_size) * factor, 0),
        halving_sum(weight_grad.reshape(local_heads, head_size, model_width) * factor, 2),
        halving_sum(grad_w_in * factor, 0),
        halving_sum(grad_w_out * factor, 1),
    )
    in_full = lax.dynamic_update_slice_in_dim(
        jnp.zeros((hidden * tensor_count,), jnp.float32), grad_b_in, tensor_rank * hidden, 0
    )
    joint_full = lax.dynamic_update_slice_in_dim(
        jnp.zeros((2, local_width * tensor_count), jnp.float32),
        grad_b_qv,
        tensor_rank * local_width,
        1,
    )
    shard_count = group_count * lax.axis_size("dp")
    vectors = (
        grad_ln1_gain,
        grad_ln1_bias,
        grad_b_o,
        grad_ln2_gain,
        grad_ln2_bias,
        grad_b_out,
        joint_full[0],
        joint_full[1],
        in_full,
    )
    pieces = [
        jnp.transpose((item * factor).reshape(shard_count, tensor_count, -1), (1, 0, 2))
        for item in vectors
    ]
    widths = [piece.shape[2] for piece in pieces]
    packed = jnp.concatenate(pieces, 2)
    packed = halving_steps(
        packed,
        0,
        [
            ("tensor", tensor_count, 8),
            ("tensor", tensor_count, 4),
            ("tensor", tensor_count, 2),
            ("tensor", tensor_count, 1),
        ],
    )
    packed = halving_steps(
        packed,
        1,
        [("group", group_count, 2), ("group", group_count, 1), ("dp", lax.axis_size("dp"), 1)],
    )
    flat = packed.reshape(-1)
    parts = []
    offset = 0
    for width in widths:
        parts.append(flat[offset : offset + width])
        offset += width
    return (
        output,
        input_grad,
        parts[0],
        parts[1],
        summed[0],
        jnp.stack((parts[6], parts[7])),
        summed[1],
        parts[2],
        parts[3],
        parts[4],
        summed[2],
        parts[8],
        summed[3],
        parts[5],
    )


def halving_steps(value, dim, steps, send_type=None):
    for axis, size, bit in steps:
        half = value.shape[dim] // 2
        low_half = lax.slice_in_dim(value, 0, half, axis=dim)
        high_half = lax.slice_in_dim(value, half, 2 * half, axis=dim)
        upper = lax.axis_index(axis) // bit % 2 == 1
        keep = jnp.where(upper, high_half, low_half)
        send = jnp.where(upper, low_half, high_half)
        if send_type is not None:
            send = send.astype(send_type)
        got = lax.ppermute(send, axis, [(i, i ^ bit) for i in range(size)])
        value = keep + got.astype(keep.dtype)
    return value


def halving_sum(value, dim):
    shape = value.shape
    groups = lax.axis_size("group")
    dps = lax.axis_size("dp")
    split = shape[:dim] + (groups * dps, shape[dim] // (groups * dps)) + shape[dim + 1 :]
    value = value.reshape(split)
    value = halving_steps(
        value, dim, [("group", groups, 2), ("group", groups, 1), ("dp", dps, 1)], jnp.bfloat16
    )
    return value.reshape(shape[:dim] + (shape[dim] // (groups * dps),) + shape[dim + 1 :])


def solution(mesh):
    in_specs = (
        P("tensor", ("group", "dp"), None),
        P("tensor", ("group", "dp"), None),
        P(),
        P(),
        P(),
        P(None, None, "tensor", None),
        P(None, "tensor"),
        P("tensor", None, None),
        P(),
        P(),
        P(),
        P(None, "tensor"),
        P("tensor"),
        P("tensor", None),
        P(),
    )
    out_specs = (
        P("tensor", ("group", "dp"), None),
        P("tensor", ("group", "dp"), None),
        P(("group", "dp", "tensor")),
        P(("group", "dp", "tensor")),
        P(("group", "dp"), None, "tensor", None),
        P(None, ("group", "dp", "tensor")),
        P("tensor", None, ("group", "dp")),
        P(("group", "dp", "tensor")),
        P(("group", "dp", "tensor")),
        P(("group", "dp", "tensor")),
        P(("group", "dp"), "tensor"),
        P(("group", "dp", "tensor")),
        P("tensor", ("group", "dp")),
        P(("group", "dp", "tensor")),
    )
    return jax.shard_map(shards, mesh=mesh, in_specs=in_specs, out_specs=out_specs, check_vma=False)
```

profile of v0, /device:TPU:0, one launch (start us, length us, event | category | flops | bytes accessed | tf_op | source)
XLA Modules:
  0.0 779.4 jit_solution(8731599573753859071)
XLA Ops:
  14.2 2.6 convert_reduce_fusion.5
  16.9 2.7 copy.44
  20.3 65.2 %all-gather.5.cloned.1.call-done = bf16[2048,1,2048]{2,0,1:T(8,128)(2,1)} async-done(((bf16[128,1,2048]{2,0,1:T(8,128)(2,1)}), bf16[2048,1,2048]{2,0,1:T(8,128)(2,1)}) %all-gather.5.cloned.1.call-update) | async-done | bytes 8388624 | tf_op jit(solution)/shard_map/all_gather | solution.py:132
  85.5 7.4 fusion.33
  93.0 3.9 fusion.127
  98.0 4.2 online-softmax.3
  103.2 5.2 fusion.126
  108.4 4.0 online-softmax.2
  113.4 5.2 fusion.125
  118.6 4.0 online-softmax.1
  123.6 4.8 fusion.124
  128.4 4.4 online-softmax
  133.8 5.6 convert_bitcast_fusion.3
  139.4 19.1 %all-gather.7.cloned.1.call-done = bf16[2048,1,2048]{2,0,1:T(8,128)(2,1)} async-done(((bf16[128,1,2048]{2,0,1:T(8,128)(2,1)}), bf16[2048,1,2048]{2,0,1:T(8,128)(2,1)}) %all-gather.7.cloned.1.call-update) | async-done | bytes 8388624 | tf_op jit(solution)/shard_map/all_gather | solution.py:167
  158.6 88.1 %reduce-scatter.5.cloned.1.call-done = bf16[128,1,2048]{2,0,1:T(8,128)(2,1)} async-done(((bf16[2048,1,2048]{2,0,1:T(8,128)(2,1)}), bf16[128,1,2048]{2,0,1:T(8,128)(2,1)}) %reduce-scatter.5.cloned.1.call-update) | async-done | bytes 524304 | tf_op jit(solution)/shard_map/reduce_scatter | solution.py:173
  251.7 70.2 %all-gather.9.cloned.1.call-done = bf16[2048,1,2048]{2,0,1:T(8,128)(2,1)} async-done(((bf16[128,1,2048]{2,0,1:T(8,128)(2,1)}), bf16[2048,1,2048]{2,0,1:T(8,128)(2,1)}) %all-gather.9.cloned.1.call-update) | async-done | bytes 8388624 | tf_op jit(solution)/shard_map/all_gather | solution.py:180
  321.9 7.5 fusion.10
  329.4 13.1 %convert_reduce_fusion = (f32[512]{0:T(512)}, bf16[2048,512]{1,0:T(8,128)(2,1)S(1)}) fusion(f32[2048,512]{1,0:T(8,128)S(1)} %fusion.10, f32[512]{0:T(512)S(1)} %copy-done.85, bf16[512,2048]{1,0:T(8,128)(2,1)S(1)} %copy-done, bf16[2048,1,2048]{2,0,1:T(8,128)(2,1)} %all-gather.7.cloned.1.call-done), kind=kOutput, calls=%fused_computation.29 | convolution fusion | flops 4319084032 | bytes 16781312 | tf_op jit(solution)/shard_map/rsd,fd->rsf/dot_general | solution.py:195
  343.9 6.9 convert_bitcast_fusion.1
  350.9 84.8 %reduce-scatter.7.cloned.1.call-done = bf16[128,1,2048]{2,0,1:T(8,128)(2,1)} async-done(((bf16[2048,1,2048]{2,0,1:T(8,128)(2,1)}), bf16[128,1,2048]{2,0,1:T(8,128)(2,1)}) %reduce-scatter.7.cloned.1.call-update) | async-done | bytes 524304 | tf_op jit(solution)/shard_map/reduce_scatter | solution.py:209
  441.7 3.0 exponential_reduce_fusion
  450.4 15.8 %convert_bitcast_fusion.2 = bf16[2048,1,2048]{2,0,1:T(8,128)(2,1)} fusion(bf16[512,2048]{1,0:T(8,128)(2,1)S(1)} %copy-done, f32[2048,512]{1,0:T(8,128)S(1)} %copy-done.89, f32[512]{0:T(512)S(1)} %copy-done.85), kind=kOutput, calls=%fused_computation.18 | convolution fusion | flops 4309647360 | bytes 14682112 | tf_op jit(solution)/shard_map/rsf,fd->rsd/dot_general | solution.py:190
  466.2 45.6 %all-gather.11.cloned.1.call-done = bf16[2048,1,2048]{2,0,1:T(8,128)(2,1)} async-done(((bf16[128,1,2048]{2,0,1:T(8,128)(2,1)}), bf16[2048,1,2048]{2,0,1:T(8,128)(2,1)}) %all-gather.11.cloned.1.call-update) | async-done | bytes 8388624 | tf_op jit(solution)/shard_map/all_gather | solution.py:223
  511.8 5.8 fusion.45
  517.6 2.7 fusion.102
  520.3 4.0 fusion.105
  524.3 3.9 fusion.108
  530.8 10.9 %multiply_reduce_fusion = (f32[512]{0:T(512)}, f32[512]{0:T(512)}, f32[512]{0:T(512)}, f32[512]{0:T(512)}, f32[512,2048]{1,0:T(8,128)}) fusion(f32[512,2048]{1,0:T(8,128)S(1)} %copy-done.2, f32[512]{0:T(512)S(1)} %copy-done.59, pred[2048]{0:T(1024)(128)(4,1)S(1)} %iota_compare_fusion.4, s32[512]{0:T(512)S(1)} %copy-done.52, f32[512,2048]{1,0:T(8,128)} %fusion.108, ...), kind=kOutput, calls=%fused_computation.31 | convolution fusion | flops 293599232 | bytes 34234368 | tf_op jit(solution)/shard_map/while/body/eval_jaxpr/dot_general | solution.py:65
  541.7 9.5 %multiply_convert_fusion = (bf16[512,2048]{1,0:T(8,128)(2,1)S(1)}, bf16[512,2048]{1,0:T(8,128)(2,1)}, bf16[512,2048]{1,0:T(8,128)(2,1)S(1)}) fusion(f32[512,2048]{1,0:T(8,128)} %get-tuple-element.119, f32[512]{0:T(512)} %get-tuple-element.82, f32[512,2048]{1,0:T(8,128)S(1)} %copy-done.2, f32[512]{0:T(512)} %get-tuple-element.124, ...), kind=kLoop, calls=%fused_computation.30 | loop fusion | flops 22020096 | bytes 31475712 | tf_op jit(solution)/shard_map/while/body/eval_jaxpr/convert_element_type | solution.py:69
  569.4 9.7 %convert_bitcast_fusion = bf16[2048,1,2048]{2,0,1:T(8,128)(2,1)} fusion(bf16[2048,384]{0,1:T(8,128)(2,1)} %bitcast.201, bf16[2048,384]{0,1:T(8,128)(2,1)} %bitcast.202), kind=kOutput, calls=%fused_computation.16 | convolution fusion | flops 3225419776 | bytes 11534336 | tf_op jit(solution)/shard_map/rsc,dc->rsd/dot_general | solution.py:250
  582.5 8.5 %fusion.27 = f32[512,2048]{1,0:T(8,128)S(1)} fusion(bf16[2048,1,2048]{2,0,1:T(8,128)(2,1)} %all-gather.7.cloned.1.call-done, f32[]{:T(128)S(6)} %div.167, f32[2048,512]{1,0:T(8,128)} %copy-done.88, f32[512]{0:T(512)S(1)} %copy-done.86), kind=kOutput, calls=%fused_computation.59 | convolution fusion | flops 4306501632 | bytes 16779268 | tf_op jit(solution)/shard_map/rsf,rsd->fd/dot_general | solution.py:194
  591.0 4.0 copy.76
  596.6 7.1 fusion.30
  611.6 2.7 slice_select_fusion
  614.4 17.2 %collective-permute-done.13 = bf16[4,256,512]{2,1,0:T(8,128)(2,1)} collective-permute-done((bf16[4,256,512]{2,1,0:T(8,128)(2,1)}, bf16[4,256,512]{2,1,0:T(8,128)(2,1)}, u32[]{:S(2)}, u32[]{:S(2)}) %collective-permute-start.13) | collective-permute-done | bytes 1048608 | tf_op jit(solution)/shard_map/ppermute | solution.py:342
  633.4 19.6 %collective-permute-done.16 = bf16[512,4,256]{2,0,1:T(8,128)(2,1)} collective-permute-done((bf16[512,4,256]{2,0,1:T(8,128)(2,1)}, bf16[512,4,256]{2,0,1:T(8,128)(2,1)}, u32[]{:S(2)}, u32[]{:S(2)}) %collective-permute-start.16) | collective-permute-done | bytes 1048608 | tf_op jit(solution)/shard_map/ppermute | solution.py:342
  656.2 3.2 collective-permute-start.15
  661.9 5.2 collective-permute-done.15
  668.0 4.4 collective-permute-done.18
  676.4 4.7 fusion.42
  683.5 7.0 fusion.36
  694.4 3.1 collective-permute-start.12
  706.6 3.1 collective-permute-start
  709.7 26.8 %collective-permute-done.7 = bf16[4,256,3,1,128]{4,3,2,1,0:T(2,128)(2,1)} collective-permute-done((bf16[4,256,3,1,128]{4,3,2,1,0:T(2,128)(2,1)S(1)}, bf16[4,256,3,1,128]{4,3,2,1,0:T(2,128)(2,1)}, u32[]{:S(2)}, u32[]{:S(2)}) %collective-permute-start.7) | collective-permute-done | bytes 786464 | tf_op jit(solution)/shard_map/ppermute | solution.py:342
  736.5 4.7 copy_add_fusion
  745.9 3.2 collective-permute-start.2
  755.1 7.4 collective-permute-done.9
  765.8 3.4 add_convert_fusion
  (355 shorter events, 106.8 us)
Async XLA Ops:
  7.2 322.2 %copy-start = (bf16[512,2048]{1,0:T(8,128)(2,1)S(1)}, bf16[512,2048]{1,0:T(8,128)(2,1)}, u32[]{:S(2)}) copy-start(bf16[512,2048]{1,0:T(8,128)(2,1)} %param.28) | copy-start | bytes 6291460
  7.2 78.3 %all-gather.5.cloned.1.call-start = ((), (), s32[]{:S(2)}) async-start(), calls=%async_computation.4 | async-start | bytes 8912896 | tf_op jit(solution)/shard_map/all_gather | solution.py:132
  8.6 84.3 %copy-start.64 = (f32[128]{0:T(128)}, f32[128]{0:T(128)S(1)}, u32[]{:S(2)}) copy-start(f32[128]{0:T(128)S(1)} %broadcast_multiply_fusion.8) | copy-start | bytes 1540
  9.9 82.9 %copy-start.73 = (f32[128]{0:T(128)}, f32[128]{0:T(128)S(1)}, u32[]{:S(2)}) copy-start(f32[128]{0:T(128)S(1)} %fusion.116) | copy-start | bytes 1540
  12.2 146.3 %all-gather.7.cloned.1.call-start = ((), (), s32[]{:S(2)}) async-start(), calls=%async_computation.5 | async-start | bytes 8912896 | tf_op jit(solution)/shard_map/all_gather | solution.py:167
  16.8 229.8 %reduce-scatter.5.cloned.1.call-start = ((), (), s32[]{:S(2)}) async-start(), calls=%async_computation.6 | async-start | bytes 8912896 | tf_op jit(solution)/shard_map/reduce_scatter | solution.py:173
  20.2 93.1 %copy-start.54 = (s32[512]{0:T(512)}, s32[512]{0:T(512)S(1)}, u32[]{:S(2)}) copy-start(s32[512]{0:T(512)S(1)} %iota_add_fusion.2) | copy-start | bytes 6148
  20.3 72.7 %copy-start.51 = (s32[512]{0:T(512)}, s32[512]{0:T(512)S(1)}, u32[]{:S(2)}) copy-start(s32[512]{0:T(512)S(1)} %iota_add_fusion) | copy-start | bytes 6148
  20.3 76.6 %copy-start.75 = (f32[128]{0:T(128)}, f32[128]{0:T(128)S(1)}, u32[]{:S(2)}) copy-start(f32[128]{0:T(128)S(1)} %get-tuple-element.109) | copy-start | bytes 1540
  93.0 30.6 %copy-start.25 = (bf16[2048,1,128]{2,0,1:T(8,128)(2,1)}, bf16[2048,1,128]{2,0,1:T(8,128)(2,1)S(1)}, u32[]{:S(2)}) copy-start(bf16[2048,1,128]{2,0,1:T(8,128)(2,1)S(1)} %fusion.83) | copy-start | bytes 1572868
  103.1 30.6 %copy-start.28 = (bf16[512,128]{1,0:T(8,128)(2,1)}, bf16[512,128]{1,0:T(8,128)(2,1)S(1)}, u32[]{:S(2)}) copy-start(bf16[512,128]{1,0:T(8,128)(2,1)S(1)} %convert_element_type.298) | copy-start | bytes 393220
  139.4 107.3 %copy-start.9 = (bf16[128,1,2048]{2,0,1:T(8,128)(2,1)S(1)}, bf16[128,1,2048]{2,0,1:T(8,128)(2,1)}, u32[]{:S(2)}) copy-start(bf16[128,1,2048]{2,0,1:T(8,128)(2,1)} %param.15) | copy-start | bytes 1572868
  139.4 107.3 %copy-start.39 = (f32[2048]{0:T(1024)S(1)}, f32[2048]{0:T(1024)}, u32[]{:S(2)}) copy-start(f32[2048]{0:T(1024)} %param.23) | copy-start | bytes 24580
  139.4 110.0 %copy-start.47 = (f32[2048]{0:T(1024)S(1)}, f32[2048]{0:T(1024)}, u32[]{:S(2)}) copy-start(f32[2048]{0:T(1024)} %param.24) | copy-start | bytes 24580
  139.4 110.0 %copy-start.70 = (f32[2048]{0:T(1024)S(1)}, f32[2048]{0:T(1024)}, u32[]{:S(2)}) copy-start(f32[2048]{0:T(1024)} %param.25) | copy-start | bytes 24580
  158.6 163.3 %all-gather.9.cloned.1.call-start = ((), (), s32[]{:S(2)}) async-start(), calls=%async_computation.7 | async-start | bytes 8912896 | tf_op jit(solution)/shard_map/all_gather | solution.py:180
  251.6 77.8 %copy-start.85 = (f32[512]{0:T(512)S(1)}, f32[512]{0:T(512)}, u32[]{:S(2)}) copy-start(f32[512]{0:T(512)} %param.27) | copy-start | bytes 6148
  251.6 184.1 %reduce-scatter.7.cloned.1.call-start = ((), (), s32[]{:S(2)}) async-start(), calls=%async_computation.8 | async-start | bytes 8912896 | tf_op jit(solution)/shard_map/reduce_scatter | solution.py:209
  350.8 84.9 %copy-start.12 = (bf16[128,1,2048]{2,0,1:T(8,128)(2,1)S(1)}, bf16[128,1,2048]{2,0,1:T(8,128)(2,1)}, u32[]{:S(2)}) copy-start(bf16[128,1,2048]{2,0,1:T(8,128)(2,1)} %reduce-scatter.5.cloned.1.call-done) | copy-start | bytes 1572868
  350.8 90.8 %copy-start.66 = (f32[512]{0:T(512)S(1)}, f32[512]{0:T(512)}, u32[]{:S(2)}) copy-start(f32[512]{0:T(512)} %get-tuple-element.117) | copy-start | bytes 6148
  350.9 160.9 %all-gather.11.cloned.1.call-start = ((), (), s32[]{:S(2)}) async-start(), calls=%async_computation.9 | async-start | bytes 8912896 | tf_op jit(solution)/shard_map/all_gather | solution.py:223
  441.6 260.6 %reduce-scatter.11.cloned.1.call-start = ((), (), s32[]{:S(2)}) async-start(), calls=%async_computation.11 | async-start | bytes 8912896 | tf_op jit(solution)/shard_map/reduce_scatter | solution.py:249
  450.4 67.2 %copy-start.19 = (bf16[2048,128]{1,0:T(8,128)(2,1)}, bf16[2048,128]{1,0:T(8,128)(2,1)S(1)}, u32[]{:S(2)}) copy-start(bf16[2048,128]{1,0:T(8,128)(2,1)S(1)} %fusion.90) | copy-start | bytes 1572868
  579.1 186.7 %reduce-scatter.9.cloned.1.call-start = ((), (), s32[]{:S(2)}) async-start(), calls=%async_computation.10 | async-start | bytes 8912896 | tf_op jit(solution)/shard_map/reduce_scatter | solution.py:226
  605.1 26.5 %collective-permute-start.13 = (bf16[4,256,512]{2,1,0:T(8,128)(2,1)}, bf16[4,256,512]{2,1,0:T(8,128)(2,1)}, u32[]{:S(2)}, u32[]{:S(2)}) collective-permute-start(bf16[4,256,512]{2,1,0:T(8,128)(2,1)} %bitcast.57), channel_id=1, source_target_pairs={{0,64},{32,96},{64,0},{96,32},{1,65},{33,97},{65,1},{97,33},{2,66}... | collective-permute-start | bytes 3145736 | tf_op jit(solution)/shard_map/ppermute | solution.py:342
  610.4 42.5 %collective-permute-start.16 = (bf16[512,4,256]{2,0,1:T(8,128)(2,1)}, bf16[512,4,256]{2,0,1:T(8,128)(2,1)}, u32[]{:S(2)}, u32[]{:S(2)}) collective-permute-start(bf16[512,4,256]{2,0,1:T(8,128)(2,1)} %select_convert_fusion), channel_id=1, source_target_pairs={{0,64},{32,96},{64,0},{96,32},{1,65},{33,97},{65,1},{97,33},{2,66}... | collective-permute-start | bytes 3145736 | tf_op jit(solution)/shard_map/ppermute | solution.py:342
  614.4 38.6 %copy-start.15 = (f32[512,4,256]{2,1,0:T(4,128)S(1)}, f32[512,4,256]{2,1,0:T(4,128)}, u32[]{:S(2)}) copy-start(f32[512,4,256]{2,1,0:T(4,128)} %copy-done.14) | copy-start | bytes 6291460
  633.3 21.9 %collective-permute-start.14 = (bf16[2,256,512]{2,1,0:T(8,128)(2,1)S(1)}, bf16[2,256,512]{2,1,0:T(8,128)(2,1)S(1)}, u32[]{:S(2)}, u32[]{:S(2)}) collective-permute-start(bf16[2,256,512]{2,1,0:T(8,128)(2,1)S(1)} %select_convert_fusion.4), channel_id=1, source_target_pairs={{0,32},{32,0},{64,96},{96,64},{1,33},{33,1},{65,97},{97,65},{2,34}... | collective-permute-start | bytes 1572872 | tf_op jit(solution)/shard_map/ppermute | solution.py:342
  655.0 4.4 collective-permute-start.17
  656.2 10.9 %collective-permute-start.15 = (bf16[1,256,512]{2,1,0:T(8,128)(2,1)}, bf16[1,256,512]{2,1,0:T(8,128)(2,1)S(1)}, u32[]{:S(2)}, u32[]{:S(2)}) collective-permute-start(bf16[1,256,512]{2,1,0:T(8,128)(2,1)} %select_convert_fusion.6), channel_id=1, source_target_pairs={{0,16},{16,0},{1,17},{17,1},{2,18},{18,2},{3,19},{19,3},{4,20},{20... | collective-permute-start | bytes 786440 | tf_op jit(solution)/shard_map/ppermute | solution.py:342
  660.4 12.0 %collective-permute-start.18 = (bf16[512,1,256]{2,0,1:T(8,128)(2,1)}, bf16[512,1,256]{2,0,1:T(8,128)(2,1)}, u32[]{:S(2)}, u32[]{:S(2)}) collective-permute-start(bf16[512,1,256]{2,0,1:T(8,128)(2,1)} %select_convert_fusion.5), channel_id=1, source_target_pairs={{0,16},{16,0},{1,17},{17,1},{2,18},{18,2},{3,19},{19,3},{4,20},{20... | collective-permute-start | bytes 786440 | tf_op jit(solution)/shard_map/ppermute | solution.py:342
  681.8 10.1 %collective-permute-start.10 = (bf16[1,128,4,256]{3,1,2,0:T(8,128)(2,1)S(1)}, bf16[1,128,4,256]{3,1,2,0:T(8,128)(2,1)S(1)}, u32[]{:S(2)}, u32[]{:S(2)}) collective-permute-start(bf16[1,128,4,256]{3,1,2,0:T(8,128)(2,1)S(1)} %select_convert_fusion.7), channel_id=1, source_target_pairs={{0,64},{32,96},{64,0},{96,32},{1,65},{33,97},{65,1},{97,33},{2,66}... | collective-permute-start | bytes 786440 | tf_op jit(solution)/shard_map/ppermute | solution.py:342
  692.2 1.4 collective-permute-start.11
  694.4 6.3 collective-permute-start.12
  700.2 36.4 %collective-permute-start.7 = (bf16[4,256,3,1,128]{4,3,2,1,0:T(2,128)(2,1)S(1)}, bf16[4,256,3,1,128]{4,3,2,1,0:T(2,128)(2,1)}, u32[]{:S(2)}, u32[]{:S(2)}) collective-permute-start(bf16[4,256,3,1,128]{4,3,2,1,0:T(2,128)(2,1)S(1)} %copy.55), channel_id=1, source_target_pairs={{0,64},{32,96},{64,0},{96,32},{1,65},{33,97},{65,1},{97,33},{2,66}... | collective-permute-start | bytes 2359304 | tf_op jit(solution)/shard_map/ppermute | solution.py:342
  706.6 34.6 %collective-permute-start = (f32[8,8,192]{2,0,1:T(8,128)S(1)}, f32[8,8,192]{2,0,1:T(8,128)S(1)}, u32[]{:S(2)}, u32[]{:S(2)}) collective-permute-start(f32[8,8,192]{2,0,1:T(8,128)S(1)} %slice_select_fusion.2), channel_id=1, source_target_pairs={{0,8},{1,9},{2,10},{3,11},{4,12},{5,13},{6,14},{7,15},{8,0},{9,1},... | collective-permute-start | bytes 147464 | tf_op jit(solution)/shard_map/ppermute | solution.py:342
  741.3 24.6 %copy-start.13 = (bf16[128,1,2048]{2,0,1:T(8,128)(2,1)S(1)}, bf16[128,1,2048]{2,0,1:T(8,128)(2,1)}, u32[]{:S(2)}) copy-start(bf16[128,1,2048]{2,0,1:T(8,128)(2,1)} %reduce-scatter.5.cloned.1.call-done) | copy-start | bytes 1572868
  741.3 24.6 %copy-start.71 = (f32[2048]{0:T(1024)S(1)}, f32[2048]{0:T(1024)}, u32[]{:S(2)}) copy-start(f32[2048]{0:T(1024)} %param.29) | copy-start | bytes 24580
  741.3 24.6 %copy-start.78 = (f32[128]{0:T(128)S(1)}, f32[128]{0:T(128)}, u32[]{:S(2)}) copy-start(f32[128]{0:T(128)} %copy-done.77) | copy-start | bytes 1540
  741.3 4.5 collective-permute-start.1
  743.6 5.4 collective-permute-start.8
  745.9 5.4 collective-permute-start.2
  749.1 23.1 %copy-start.1 = (bf16[512,2048]{1,0:T(8,128)(2,1)S(1)}, bf16[512,2048]{1,0:T(8,128)(2,1)}, u32[]{:S(2)}) copy-start(bf16[512,2048]{1,0:T(8,128)(2,1)} %param.28) | copy-start | bytes 6291460
  751.3 3.7 collective-permute-start.3
  753.2 9.4 %collective-permute-start.9 = (bf16[1,256,3,1,128]{4,3,2,1,0:T(2,128)(2,1)S(1)}, bf16[1,256,3,1,128]{4,3,2,1,0:T(2,128)(2,1)S(1)}, u32[]{:S(2)}, u32[]{:S(2)}) collective-permute-start(bf16[1,256,3,1,128]{4,3,2,1,0:T(2,128)(2,1)S(1)} %fusion.96), channel_id=1, source_target_pairs={{0,16},{16,0},{1,17},{17,1},{2,18},{18,2},{3,19},{19,3},{4,20},{20... | collective-permute-start | bytes 589832 | tf_op jit(solution)/shard_map/ppermute | solution.py:342
  755.1 9.0 %collective-permute-start.4 = (f32[1,4,192]{2,0,1:T(1,128)S(1)}, f32[1,4,192]{2,0,1:T(1,128)S(1)}, u32[]{:S(2)}, u32[]{:S(2)}) collective-permute-start(f32[1,4,192]{2,0,1:T(1,128)S(1)} %broadcast_select_fusion.8), channel_id=1, source_target_pairs={{0,64},{32,96},{64,0},{96,32},{1,65},{33,97},{65,1},{97,33},{2,66}... | collective-permute-start | bytes 9224 | tf_op jit(solution)/shard_map/ppermute | solution.py:342
  764.0 1.2 collective-permute-start.5
  765.3 5.2 collective-permute-start.6
  (71 other events, 508.9 us)
Sparse Core Ops, SparseCore 0:
  12.4 73.0 all-gather.4
  88.2 70.3 all-gather.6
  162.0 84.6 reduce-scatter.4
  251.8 70.0 all-gather.8
  351.0 84.6 reduce-scatter.6
  441.7 70.0 all-gather.10
  579.2 84.8 reduce-scatter.10
  667.6 85.7 reduce-scatter.8
where the time goes:
time: 789 us; the launch traced here: 779 us
  waiting for transfers between devices  461 us (58%)
  matrix products  155 us (20%)
  other arithmetic  78.1 us (10%)
  local copies, waits for them, and re-layouts  28.2 us (4%)
  starting transfers between devices  22.8 us (3%)
  between operations  17.3 us (2%)
  Pallas kernels  16.6 us (2%)
    ppermute x19, waiting for transfers between devices, halving_steps(): got = lax.ppermute(send, axis, [(i, i ^ bit) for i in range(size)])  88.2 us
    reduce_scatter x1, waiting for transfers between devices, shards(): lax.psum_scatter(attention_part, 'tensor', scatter_dimension=0, tiled=True)  88.1 us
    reduce_scatter x1, waiting for transfers between devices, shards(): lax.psum_scatter(jnp.einsum('rsf,df->rsd', piece, w_in, preferred_element...  84.8 us
    all_gather x1, waiting for transfers between devices, shards(): second_full = lax.all_gather(second_low, 'tensor', axis=0, tiled=True)  70.2 us
    all_gather x1, waiting for transfers between devices, shards(): normed_full = lax.all_gather(normed_low, 'tensor', axis=0, tiled=True)  65.2 us
    all_gather x1, waiting for transfers between devices, shards(): piece = lax.all_gather(branch_low, 'tensor', axis=0, tiled=True)  45.6 us
    ppermute x19, starting transfers between devices, halving_steps(): got = lax.ppermute(send, axis, [(i, i ^ bit) for i in range(size)])  22.5 us
    dot_general x4, matrix products, attend_backward(): lax.dot_general(grad_rows, value_rows, (((1,), (1,)), ((), ())), preferre...  21.5 us
  transfers between devices with their start and end apart: 27, of which 19 were waited for; matrix products, arithmetic and copies ran while one was open for 18% of the time, Pallas kernels for 2%

commit v1 on v0

--- a/solution.py
+++ b/solution.py
@@ -1,3 +1,4 @@
+import functools
 from functools import partial
 import math
 import jax
@@ -7,6 +8,23 @@
 
 EPS = 1e-05
 NEGATIVE = -1e30
+
+
+def seats_all_start(sheet, bus_axis, where_dim):
+    vals = [sheet]
+    extent = lax.psum(1, bus_axis)
+    for src_i in range(extent - 1):
+        vals.append(
+            lax.ppermute(vals[-1], bus_axis, [(it, (it + 1) % extent) for it in range(extent)])
+        )
+    return jnp.roll(
+        jnp.concatenate(vals[::-1], axis=where_dim),
+        (lax.axis_index(bus_axis) + 1) * sheet.shape[where_dim],
+        axis=where_dim,
+    )
+
+
+_supply_modes = functools.partial(seats_all_start, bus_axis="tensor", where_dim=0)
 
 
 def layer_norm(value, gain, shift):
@@ -177,7 +195,7 @@
     )
     middle = inputs + attention
     second_low = layer_norm(middle, ln2_gain, ln2_bias).astype(jnp.bfloat16)
-    second_full = lax.all_gather(second_low, "tensor", axis=0, tiled=True)
+    second_full = _supply_modes(second_low)
     pre_act = (
         jnp.dot(
             second_full.reshape(seq_total * seq_count, model_width),

time: 789 us -> 951 us (1.21)
  waiting for transfers between devices: 461 us -> 609 us
  local copies, waits for them, and re-layouts: 28.2 us -> 58 us
  matrix products: 155 us -> 138 us
    ppermute x0 -> x15, waiting for transfers between devices: none -> 222 us  [seats_all_start(): lax.ppermute(vals[-1], bus_axis, [(it, (it + 1) % extent) for it in range...]
    all_gather x1 -> x0, waiting for transfers between devices: 70.2 us -> none  [shards(): second_full = lax.all_gather(second_low, 'tensor', axis=0, tiled=True)]
    unnamed x187 -> x278, local copies, waits for them, and re-layouts: 15.3 us -> 41.4 us
  transfers between devices with their start and end apart: 27 -> 41, of which waited for: 19 -> 33; matrix products, arithmetic and copies ran while one was open for 18% -> 15% of each run, Pallas kernels for 2% -> 2%
where the time goes in v1:
time: 951 us; the launch traced here: 941 us
  waiting for transfers between devices  609 us (64%)
  matrix products  138 us (15%)
  other arithmetic  78.7 us (8%)
  local copies, waits for them, and re-layouts  58 us (6%)
  starting transfers between devices  24 us (3%)
  between operations  17.8 us (2%)
  Pallas kernels  16.6 us (2%)
    ppermute x15, waiting for transfers between devices, seats_all_start(): lax.ppermute(vals[-1], bus_axis, [(it, (it + 1) % extent) for it in range...  222 us
    reduce_scatter x1, waiting for transfers between devices, shards(): lax.psum_scatter(attention_part, 'tensor', scatter_dimension=0, tiled=True)  88.1 us
    reduce_scatter x1, waiting for transfers between devices, shards(): lax.psum_scatter(jnp.einsum('rsf,df->rsd', piece, w_in, preferred_element...  81.3 us
    ppermute x19, waiting for transfers between devices, halving_steps(): got = lax.ppermute(send, axis, [(i, i ^ bit) for i in range(size)])  80 us
    all_gather x1, waiting for transfers between devices, shards(): normed_full = lax.all_gather(normed_low, 'tensor', axis=0, tiled=True)  65.2 us
    all_gather x1, waiting for transfers between devices, shards(): piece = lax.all_gather(branch_low, 'tensor', axis=0, tiled=True)  53.2 us
    unnamed x278, local copies, waits for them, and re-layouts  41.4 us
    ppermute x19, starting transfers between devices, halving_steps(): got = lax.ppermute(send, axis, [(i, i ^ bit) for i in range(size)])  22.1 us
  transfers between devices with their start and end apart: 41, of which 33 were waited for; matrix products, arithmetic and copies ran while one was open for 15% of the time, Pallas kernels for 2%

profile of v1, /device:TPU:0, one launch (start us, length us, event | category | flops | bytes accessed | tf_op | source)
XLA Modules:
  0.0 941.5 jit_solution(2740104426344165628)
XLA Ops:
  20.3 65.2 %all-gather.4.cloned.1.call-done = bf16[2048,1,2048]{2,0,1:T(8,128)(2,1)} async-done(((bf16[128,1,2048]{2,0,1:T(8,128)(2,1)}), bf16[2048,1,2048]{2,0,1:T(8,128)(2,1)}) %all-gather.4.cloned.1.call-update) | async-done | bytes 8388624 | tf_op jit(solution)/shard_map/all_gather | solution.py:150
  85.5 7.4 fusion.35
  98.0 4.1 online-softmax.1
  103.1 5.3 fusion.130
  113.4 5.2 fusion.131
  118.6 4.2 online-softmax.3
  123.8 4.9 fusion.128
  128.7 4.2 online-softmax
  134.0 5.7 convert_bitcast_fusion.3
  139.7 18.3 %all-gather.6.cloned.1.call-done = bf16[2048,1,2048]{2,0,1:T(8,128)(2,1)} async-done(((bf16[128,1,2048]{2,0,1:T(8,128)(2,1)}), bf16[2048,1,2048]{2,0,1:T(8,128)(2,1)}) %all-gather.6.cloned.1.call-update) | async-done | bytes 8388624 | tf_op jit(solution)/shard_map/all_gather | solution.py:185
  158.0 88.1 %reduce-scatter.5.cloned.1.call-done = bf16[128,1,2048]{2,0,1:T(8,128)(2,1)} async-done(((bf16[2048,1,2048]{2,0,1:T(8,128)(2,1)}), bf16[128,1,2048]{2,0,1:T(8,128)(2,1)}) %reduce-scatter.5.cloned.1.call-update) | async-done | bytes 524304 | tf_op jit(solution)/shard_map/reduce_scatter | solution.py:191
  251.8 14.3 %collective-permute-done = bf16[128,1,2048]{2,0,1:T(8,128)(2,1)S(1)} collective-permute-done((bf16[128,1,2048]{2,0,1:T(8,128)(2,1)S(1)}, bf16[128,1,2048]{2,0,1:T(8,128)(2,1)S(1)}, u32[]{:S(2)}, u32[]{:S(2)}) %collective-permute-start) | collective-permute-done | bytes 524320 | tf_op jit(solution)/shard_map/ppermute | solution.py:18
  267.0 14.9 %collective-permute-done.1 = bf16[128,1,2048]{2,0,1:T(8,128)(2,1)S(1)} collective-permute-done((bf16[128,1,2048]{2,0,1:T(8,128)(2,1)S(1)}, bf16[128,1,2048]{2,0,1:T(8,128)(2,1)S(1)}, u32[]{:S(2)}, u32[]{:S(2)}) %collective-permute-start.1) | collective-permute-done | bytes 524320 | tf_op jit(solution)/shard_map/ppermute | solution.py:18
  282.7 14.0 %collective-permute-done.2 = bf16[128,1,2048]{2,0,1:T(8,128)(2,1)S(1)} collective-permute-done((bf16[128,1,2048]{2,0,1:T(8,128)(2,1)S(1)}, bf16[128,1,2048]{2,0,1:T(8,128)(2,1)S(1)}, u32[]{:S(2)}, u32[]{:S(2)}) %collective-permute-start.2) | collective-permute-done | bytes 524320 | tf_op jit(solution)/shard_map/ppermute | solution.py:18
  297.5 13.0 %collective-permute-done.3 = bf16[128,1,2048]{2,0,1:T(8,128)(2,1)S(1)} collective-permute-done((bf16[128,1,2048]{2,0,1:T(8,128)(2,1)S(1)}, bf16[128,1,2048]{2,0,1:T(8,128)(2,1)S(1)}, u32[]{:S(2)}, u32[]{:S(2)}) %collective-permute-start.3) | collective-permute-done | bytes 524320 | tf_op jit(solution)/shard_map/ppermute | solution.py:18
  311.3 12.5 %collective-permute-done.4 = bf16[128,1,2048]{2,0,1:T(8,128)(2,1)S(1)} collective-permute-done((bf16[128,1,2048]{2,0,1:T(8,128)(2,1)S(1)}, bf16[128,1,2048]{2,0,1:T(8,128)(2,1)S(1)}, u32[]{:S(2)}, u32[]{:S(2)}) %collective-permute-start.4) | collective-permute-done | bytes 524320 | tf_op jit(solution)/shard_map/ppermute | solution.py:18
  324.6 13.0 %collective-permute-done.5 = bf16[128,1,2048]{2,0,1:T(8,128)(2,1)S(1)} collective-permute-done((bf16[128,1,2048]{2,0,1:T(8,128)(2,1)S(1)}, bf16[128,1,2048]{2,0,1:T(8,128)(2,1)S(1)}, u32[]{:S(2)}, u32[]{:S(2)}) %collective-permute-start.5) | collective-permute-done | bytes 524320 | tf_op jit(solution)/shard_map/ppermute | solution.py:18
  338.5 14.1 %collective-permute-done.6 = bf16[128,1,2048]{2,0,1:T(8,128)(2,1)S(1)} collective-permute-done((bf16[128,1,2048]{2,0,1:T(8,128)(2,1)S(1)}, bf16[128,1,2048]{2,0,1:T(8,128)(2,1)S(1)}, u32[]{:S(2)}, u32[]{:S(2)}) %collective-permute-start.6) | collective-permute-done | bytes 524320 | tf_op jit(solution)/shard_map/ppermute | solution.py:18
  353.4 15.2 %collective-permute-done.7 = bf16[128,1,2048]{2,0,1:T(8,128)(2,1)S(1)} collective-permute-done((bf16[128,1,2048]{2,0,1:T(8,128)(2,1)S(1)}, bf16[128,1,2048]{2,0,1:T(8,128)(2,1)S(1)}, u32[]{:S(2)}, u32[]{:S(2)}) %collective-permute-start.7) | collective-permute-done | bytes 524320 | tf_op jit(solution)/shard_map/ppermute | solution.py:18
  369.4 16.3 %collective-permute-done.8 = bf16[128,1,2048]{2,0,1:T(8,128)(2,1)S(1)} collective-permute-done((bf16[128,1,2048]{2,0,1:T(8,128)(2,1)S(1)}, bf16[128,1,2048]{2,0,1:T(8,128)(2,1)S(1)}, u32[]{:S(2)}, u32[]{:S(2)}) %collective-permute-start.8) | collective-permute-done | bytes 524320 | tf_op jit(solution)/shard_map/ppermute | solution.py:18
  386.5 17.5 %collective-permute-done.9 = bf16[128,1,2048]{2,0,1:T(8,128)(2,1)S(1)} collective-permute-done((bf16[128,1,2048]{2,0,1:T(8,128)(2,1)S(1)}, bf16[128,1,2048]{2,0,1:T(8,128)(2,1)S(1)}, u32[]{:S(2)}, u32[]{:S(2)}) %collective-permute-start.9) | collective-permute-done | bytes 524320 | tf_op jit(solution)/shard_map/ppermute | solution.py:18
  404.8 17.6 %collective-permute-done.10 = bf16[128,1,2048]{2,0,1:T(8,128)(2,1)S(1)} collective-permute-done((bf16[128,1,2048]{2,0,1:T(8,128)(2,1)S(1)}, bf16[128,1,2048]{2,0,1:T(8,128)(2,1)S(1)}, u32[]{:S(2)}, u32[]{:S(2)}) %collective-permute-start.10) | collective-permute-done | bytes 524320 | tf_op jit(solution)/shard_map/ppermute | solution.py:18
  423.2 16.8 %collective-permute-done.11 = bf16[128,1,2048]{2,0,1:T(8,128)(2,1)S(1)} collective-permute-done((bf16[128,1,2048]{2,0,1:T(8,128)(2,1)S(1)}, bf16[128,1,2048]{2,0,1:T(8,128)(2,1)S(1)}, u32[]{:S(2)}, u32[]{:S(2)}) %collective-permute-start.11) | collective-permute-done | bytes 524320 | tf_op jit(solution)/shard_map/ppermute | solution.py:18
  440.8 15.9 %collective-permute-done.12 = bf16[128,1,2048]{2,0,1:T(8,128)(2,1)S(1)} collective-permute-done((bf16[128,1,2048]{2,0,1:T(8,128)(2,1)S(1)}, bf16[128,1,2048]{2,0,1:T(8,128)(2,1)S(1)}, u32[]{:S(2)}, u32[]{:S(2)}) %collective-permute-start.12) | collective-permute-done | bytes 524320 | tf_op jit(solution)/shard_map/ppermute | solution.py:18
  457.5 14.5 %collective-permute-done.13 = bf16[128,1,2048]{2,0,1:T(8,128)(2,1)} collective-permute-done((bf16[128,1,2048]{2,0,1:T(8,128)(2,1)S(1)}, bf16[128,1,2048]{2,0,1:T(8,128)(2,1)}, u32[]{:S(2)}, u32[]{:S(2)}) %collective-permute-start.13) | collective-permute-done | bytes 524320 | tf_op jit(solution)/shard_map/ppermute | solution.py:18
  472.0 12.8 %collective-permute-done.14 = bf16[128,1,2048]{2,0,1:T(8,128)(2,1)} collective-permute-done((bf16[128,1,2048]{2,0,1:T(8,128)(2,1)}, bf16[128,1,2048]{2,0,1:T(8,128)(2,1)}, u32[]{:S(2)}, u32[]{:S(2)}) %collective-permute-start.14) | collective-permute-done | bytes 524320 | tf_op jit(solution)/shard_map/ppermute | solution.py:18
  493.7 7.4 copy-done.93
  501.0 6.4 fusion.10
  507.5 9.9 %convert_reduce_fusion = (f32[512]{0:T(512)}, bf16[2048,512]{1,0:T(8,128)(2,1)S(1)}) fusion(f32[2048,512]{1,0:T(8,128)} %fusion.10, f32[512]{0:T(512)S(1)} %copy-done.115, bf16[512,2048]{1,0:T(8,128)(2,1)S(1)} %copy-done, bf16[2048,1,2048]{2,0,1:T(8,128)(2,1)S(1)} %bitcast.213), kind=kOutput, calls=%fused_computation.31 | convolution fusion | flops 4319084032 | bytes 16781312 | tf_op jit(solution)/shard_map/rsd,fd->rsf/dot_general | solution.py:213
  518.7 6.8 convert_bitcast_fusion.1
  525.6 81.3 %reduce-scatter.7.cloned.1.call-done = bf16[128,1,2048]{2,0,1:T(8,128)(2,1)} async-done(((bf16[2048,1,2048]{2,0,1:T(8,128)(2,1)}), bf16[128,1,2048]{2,0,1:T(8,128)(2,1)}) %reduce-scatter.7.cloned.1.call-update) | async-done | bytes 524304 | tf_op jit(solution)/shard_map/reduce_scatter | solution.py:227
  622.3 7.3 convert_bitcast_fusion.2
  629.7 53.2 %all-gather.8.cloned.1.call-done = bf16[2048,1,2048]{2,0,1:T(8,128)(2,1)} async-done(((bf16[128,1,2048]{2,0,1:T(8,128)(2,1)}), bf16[2048,1,2048]{2,0,1:T(8,128)(2,1)}) %all-gather.8.cloned.1.call-update) | async-done | bytes 8388624 | tf_op jit(solution)/shard_map/all_gather | solution.py:241
  682.9 5.9 fusion.47
  697.9 10.1 %multiply_reduce_fusion = (f32[512]{0:T(512)}, f32[512]{0:T(512)}, f32[512]{0:T(512)}, f32[512]{0:T(512)}, f32[512,2048]{1,0:T(8,128)}) fusion(f32[512,2048]{1,0:T(8,128)S(1)} %copy-done.4, f32[512]{0:T(512)S(1)} %copy-done.87, pred[2048]{0:T(1024)(128)(4,1)S(1)} %iota_compare_fusion.4, s32[512]{0:T(512)S(1)} %iota_add_fusion, f32[512,2048]{1,0:T(8,128)} %fusion.110, ...), kind=kOutput, calls=%fused_computation.33 | convolution fusion | flops 293599232 | bytes 34234368 | tf_op jit(solution)/shard_map/while/body/eval_jaxpr/dot_general | solution.py:83
  708.0 9.3 multiply_convert_fusion
  736.3 9.7 %convert_bitcast_fusion = bf16[2048,1,2048]{2,0,1:T(8,128)(2,1)} fusion(bf16[2048,384]{0,1:T(8,128)(2,1)} %bitcast.202, bf16[2048,384]{0,1:T(8,128)(2,1)} %bitcast.201), kind=kOutput, calls=%fused_computation.16 | convolution fusion | flops 3225419776 | bytes 11534336 | tf_op jit(solution)/shard_map/rsc,dc->rsd/dot_general | solution.py:268
  749.5 8.5 fusion.29
  762.1 4.3 fusion.126
  769.6 7.4 fusion.32
  784.1 10.3 %collective-permute-done.31 = bf16[512,4,256]{2,0,1:T(8,128)(2,1)} collective-permute-done((bf16[512,4,256]{2,0,1:T(8,128)(2,1)}, bf16[512,4,256]{2,0,1:T(8,128)(2,1)}, u32[]{:S(2)}, u32[]{:S(2)}) %collective-permute-start.31) | collective-permute-done | bytes 1048608 | tf_op jit(solution)/shard_map/ppermute | solution.py:360
  796.5 19.2 %collective-permute-done.28 = bf16[4,256,512]{2,1,0:T(8,128)(2,1)} collective-permute-done((bf16[4,256,512]{2,1,0:T(8,128)(2,1)}, bf16[4,256,512]{2,1,0:T(8,128)(2,1)}, u32[]{:S(2)}, u32[]{:S(2)}) %collective-permute-start.28) | collective-permute-done | bytes 1048608 | tf_op jit(solution)/shard_map/ppermute | solution.py:360
  824.6 4.9 collective-permute-done.33
  839.0 4.7 fusion.44
  846.0 7.0 fusion.38
  872.3 26.7 %collective-permute-done.22 = bf16[4,256,3,1,128]{4,3,2,1,0:T(2,128)(2,1)} collective-permute-done((bf16[4,256,3,1,128]{4,3,2,1,0:T(2,128)(2,1)S(1)}, bf16[4,256,3,1,128]{4,3,2,1,0:T(2,128)(2,1)}, u32[]{:S(2)}, u32[]{:S(2)}) %collective-permute-start.22) | collective-permute-done | bytes 786464 | tf_op jit(solution)/shard_map/ppermute | solution.py:360
  899.0 4.3 copy_add_fusion
  917.2 7.5 collective-permute-done.24
  (475 shorter events, 176.8 us)
Async XLA Ops:
  7.2 500.3 %copy-start = (bf16[512,2048]{1,0:T(8,128)(2,1)S(1)}, bf16[512,2048]{1,0:T(8,128)(2,1)}, u32[]{:S(2)}) copy-start(bf16[512,2048]{1,0:T(8,128)(2,1)} %param.28) | copy-start | bytes 6291460
  7.2 78.3 %all-gather.4.cloned.1.call-start = ((), (), s32[]{:S(2)}) async-start(), calls=%async_computation.4 | async-start | bytes 8912896 | tf_op jit(solution)/shard_map/all_gather | solution.py:150
  8.6 84.3 %copy-start.94 = (f32[128]{0:T(128)}, f32[128]{0:T(128)S(1)}, u32[]{:S(2)}) copy-start(f32[128]{0:T(128)S(1)} %broadcast_multiply_fusion.8) | copy-start | bytes 1540
  12.2 145.7 %all-gather.6.cloned.1.call-start = ((), (), s32[]{:S(2)}) async-start(), calls=%async_computation.5 | async-start | bytes 8912896 | tf_op jit(solution)/shard_map/all_gather | solution.py:185
  16.8 229.3 %reduce-scatter.5.cloned.1.call-start = ((), (), s32[]{:S(2)}) async-start(), calls=%async_computation.6 | async-start | bytes 8912896 | tf_op jit(solution)/shard_map/reduce_scatter | solution.py:191
  139.6 106.5 %copy-start.9 = (bf16[128,1,2048]{2,0,1:T(8,128)(2,1)S(1)}, bf16[128,1,2048]{2,0,1:T(8,128)(2,1)}, u32[]{:S(2)}) copy-start(bf16[128,1,2048]{2,0,1:T(8,128)(2,1)} %param.15) | copy-start | bytes 1572868
  139.6 106.5 %copy-start.67 = (f32[2048]{0:T(1024)S(1)}, f32[2048]{0:T(1024)}, u32[]{:S(2)}) copy-start(f32[2048]{0:T(1024)} %param.23) | copy-start | bytes 24580
  139.6 109.2 %copy-start.75 = (f32[2048]{0:T(1024)S(1)}, f32[2048]{0:T(1024)}, u32[]{:S(2)}) copy-start(f32[2048]{0:T(1024)} %param.24) | copy-start | bytes 24580
  139.6 109.2 %copy-start.100 = (f32[2048]{0:T(1024)S(1)}, f32[2048]{0:T(1024)}, u32[]{:S(2)}) copy-start(f32[2048]{0:T(1024)} %param.25) | copy-start | bytes 24580
  158.0 448.8 %reduce-scatter.7.cloned.1.call-start = ((), (), s32[]{:S(2)}) async-start(), calls=%async_computation.7 | async-start | bytes 8912896 | tf_op jit(solution)/shard_map/reduce_scatter | solution.py:227
  250.2 15.9 %collective-permute-start = (bf16[128,1,2048]{2,0,1:T(8,128)(2,1)S(1)}, bf16[128,1,2048]{2,0,1:T(8,128)(2,1)S(1)}, u32[]{:S(2)}, u32[]{:S(2)}) collective-permute-start(bf16[128,1,2048]{2,0,1:T(8,128)(2,1)S(1)} %add_convert_fusion.3), channel_id=1, source_target_pairs={{0,1},{1,2},{2,3},{3,4},{4,5},{5,6},{6,7},{7,8},{8,9},{9,10},{10,1... | collective-permute-start | bytes 1572872 | tf_op jit(solution)/shard_map/ppermute | solution.py:18
  267.0 14.9 %collective-permute-start.1 = (bf16[128,1,2048]{2,0,1:T(8,128)(2,1)S(1)}, bf16[128,1,2048]{2,0,1:T(8,128)(2,1)S(1)}, u32[]{:S(2)}, u32[]{:S(2)}) collective-permute-start(bf16[128,1,2048]{2,0,1:T(8,128)(2,1)S(1)} %collective-permute-done), channel_id=1, source_target_pairs={{0,1},{1,2},{2,3},{3,4},{4,5},{5,6},{6,7},{7,8},{8,9},{9,10},{10,1... | collective-permute-start | bytes 1572872 | tf_op jit(solution)/shard_map/ppermute | solution.py:18
  282.7 14.0 %collective-permute-start.2 = (bf16[128,1,2048]{2,0,1:T(8,128)(2,1)S(1)}, bf16[128,1,2048]{2,0,1:T(8,128)(2,1)S(1)}, u32[]{:S(2)}, u32[]{:S(2)}) collective-permute-start(bf16[128,1,2048]{2,0,1:T(8,128)(2,1)S(1)} %collective-permute-done.1), channel_id=1, source_target_pairs={{0,1},{1,2},{2,3},{3,4},{4,5},{5,6},{6,7},{7,8},{8,9},{9,10},{10,1... | collective-permute-start | bytes 1572872 | tf_op jit(solution)/shard_map/ppermute | solution.py:18
  297.5 13.0 %collective-permute-start.3 = (bf16[128,1,2048]{2,0,1:T(8,128)(2,1)S(1)}, bf16[128,1,2048]{2,0,1:T(8,128)(2,1)S(1)}, u32[]{:S(2)}, u32[]{:S(2)}) collective-permute-start(bf16[128,1,2048]{2,0,1:T(8,128)(2,1)S(1)} %collective-permute-done.2), channel_id=1, source_target_pairs={{0,1},{1,2},{2,3},{3,4},{4,5},{5,6},{6,7},{7,8},{8,9},{9,10},{10,1... | collective-permute-start | bytes 1572872 | tf_op jit(solution)/shard_map/ppermute | solution.py:18
  311.3 12.5 %collective-permute-start.4 = (bf16[128,1,2048]{2,0,1:T(8,128)(2,1)S(1)}, bf16[128,1,2048]{2,0,1:T(8,128)(2,1)S(1)}, u32[]{:S(2)}, u32[]{:S(2)}) collective-permute-start(bf16[128,1,2048]{2,0,1:T(8,128)(2,1)S(1)} %collective-permute-done.3), channel_id=1, source_target_pairs={{0,1},{1,2},{2,3},{3,4},{4,5},{5,6},{6,7},{7,8},{8,9},{9,10},{10,1... | collective-permute-start | bytes 1572872 | tf_op jit(solution)/shard_map/ppermute | solution.py:18
  324.6 13.0 %collective-permute-start.5 = (bf16[128,1,2048]{2,0,1:T(8,128)(2,1)S(1)}, bf16[128,1,2048]{2,0,1:T(8,128)(2,1)S(1)}, u32[]{:S(2)}, u32[]{:S(2)}) collective-permute-start(bf16[128,1,2048]{2,0,1:T(8,128)(2,1)S(1)} %collective-permute-done.4), channel_id=1, source_target_pairs={{0,1},{1,2},{2,3},{3,4},{4,5},{5,6},{6,7},{7,8},{8,9},{9,10},{10,1... | collective-permute-start | bytes 1572872 | tf_op jit(solution)/shard_map/ppermute | solution.py:18
  338.5 14.1 %collective-permute-start.6 = (bf16[128,1,2048]{2,0,1:T(8,128)(2,1)S(1)}, bf16[128,1,2048]{2,0,1:T(8,128)(2,1)S(1)}, u32[]{:S(2)}, u32[]{:S(2)}) collective-permute-start(bf16[128,1,2048]{2,0,1:T(8,128)(2,1)S(1)} %collective-permute-done.5), channel_id=1, source_target_pairs={{0,1},{1,2},{2,3},{3,4},{4,5},{5,6},{6,7},{7,8},{8,9},{9,10},{10,1... | collective-permute-start | bytes 1572872 | tf_op jit(solution)/shard_map/ppermute | solution.py:18
  353.4 15.2 %collective-permute-start.7 = (bf16[128,1,2048]{2,0,1:T(8,128)(2,1)S(1)}, bf16[128,1,2048]{2,0,1:T(8,128)(2,1)S(1)}, u32[]{:S(2)}, u32[]{:S(2)}) collective-permute-start(bf16[128,1,2048]{2,0,1:T(8,128)(2,1)S(1)} %collective-permute-done.6), channel_id=1, source_target_pairs={{0,1},{1,2},{2,3},{3,4},{4,5},{5,6},{6,7},{7,8},{8,9},{9,10},{10,1... | collective-permute-start | bytes 1572872 | tf_op jit(solution)/shard_map/ppermute | solution.py:18
  369.4 16.3 %collective-permute-start.8 = (bf16[128,1,2048]{2,0,1:T(8,128)(2,1)S(1)}, bf16[128,1,2048]{2,0,1:T(8,128)(2,1)S(1)}, u32[]{:S(2)}, u32[]{:S(2)}) collective-permute-start(bf16[128,1,2048]{2,0,1:T(8,128)(2,1)S(1)} %collective-permute-done.7), channel_id=1, source_target_pairs={{0,1},{1,2},{2,3},{3,4},{4,5},{5,6},{6,7},{7,8},{8,9},{9,10},{10,1... | collective-permute-start | bytes 1572872 | tf_op jit(solution)/shard_map/ppermute | solution.py:18
  386.5 17.5 %collective-permute-start.9 = (bf16[128,1,2048]{2,0,1:T(8,128)(2,1)S(1)}, bf16[128,1,2048]{2,0,1:T(8,128)(2,1)S(1)}, u32[]{:S(2)}, u32[]{:S(2)}) collective-permute-start(bf16[128,1,2048]{2,0,1:T(8,128)(2,1)S(1)} %collective-permute-done.8), channel_id=1, source_target_pairs={{0,1},{1,2},{2,3},{3,4},{4,5},{5,6},{6,7},{7,8},{8,9},{9,10},{10,1... | collective-permute-start | bytes 1572872 | tf_op jit(solution)/shard_map/ppermute | solution.py:18
  404.8 17.6 %collective-permute-start.10 = (bf16[128,1,2048]{2,0,1:T(8,128)(2,1)S(1)}, bf16[128,1,2048]{2,0,1:T(8,128)(2,1)S(1)}, u32[]{:S(2)}, u32[]{:S(2)}) collective-permute-start(bf16[128,1,2048]{2,0,1:T(8,128)(2,1)S(1)} %collective-permute-done.9), channel_id=1, source_target_pairs={{0,1},{1,2},{2,3},{3,4},{4,5},{5,6},{6,7},{7,8},{8,9},{9,10},{10,1... | collective-permute-start | bytes 1572872 | tf_op jit(solution)/shard_map/ppermute | solution.py:18
  423.2 16.8 %collective-permute-start.11 = (bf16[128,1,2048]{2,0,1:T(8,128)(2,1)S(1)}, bf16[128,1,2048]{2,0,1:T(8,128)(2,1)S(1)}, u32[]{:S(2)}, u32[]{:S(2)}) collective-permute-start(bf16[128,1,2048]{2,0,1:T(8,128)(2,1)S(1)} %collective-permute-done.10), channel_id=1, source_target_pairs={{0,1},{1,2},{2,3},{3,4},{4,5},{5,6},{6,7},{7,8},{8,9},{9,10},{10,1... | collective-permute-start | bytes 1572872 | tf_op jit(solution)/shard_map/ppermute | solution.py:18
  440.8 15.9 %collective-permute-start.12 = (bf16[128,1,2048]{2,0,1:T(8,128)(2,1)S(1)}, bf16[128,1,2048]{2,0,1:T(8,128)(2,1)S(1)}, u32[]{:S(2)}, u32[]{:S(2)}) collective-permute-start(bf16[128,1,2048]{2,0,1:T(8,128)(2,1)S(1)} %collective-permute-done.11), channel_id=1, source_target_pairs={{0,1},{1,2},{2,3},{3,4},{4,5},{5,6},{6,7},{7,8},{8,9},{9,10},{10,1... | collective-permute-start | bytes 1572872 | tf_op jit(solution)/shard_map/ppermute | solution.py:18
  457.5 14.5 %collective-permute-start.13 = (bf16[128,1,2048]{2,0,1:T(8,128)(2,1)S(1)}, bf16[128,1,2048]{2,0,1:T(8,128)(2,1)}, u32[]{:S(2)}, u32[]{:S(2)}) collective-permute-start(bf16[128,1,2048]{2,0,1:T(8,128)(2,1)S(1)} %collective-permute-done.12), channel_id=1, source_target_pairs={{0,1},{1,2},{2,3},{3,4},{4,5},{5,6},{6,7},{7,8},{8,9},{9,10},{10,1... | collective-permute-start | bytes 1572872 | tf_op jit(solution)/shard_map/ppermute | solution.py:18
  472.0 12.8 %collective-permute-start.14 = (bf16[128,1,2048]{2,0,1:T(8,128)(2,1)}, bf16[128,1,2048]{2,0,1:T(8,128)(2,1)}, u32[]{:S(2)}, u32[]{:S(2)}) collective-permute-start(bf16[128,1,2048]{2,0,1:T(8,128)(2,1)} %collective-permute-done.13), channel_id=1, source_target_pairs={{0,1},{1,2},{2,3},{3,4},{4,5},{5,6},{6,7},{7,8},{8,9},{9,10},{10,1... | collective-permute-start | bytes 1572872 | tf_op jit(solution)/shard_map/ppermute | solution.py:18
  525.5 87.3 %copy-start.97 = (f32[512]{0:T(512)S(1)}, f32[512]{0:T(512)}, u32[]{:S(2)}) copy-start(f32[512]{0:T(512)} %get-tuple-element.113) | copy-start | bytes 6148
  525.5 157.4 %all-gather.8.cloned.1.call-start = ((), (), s32[]{:S(2)}) async-start(), calls=%async_computation.8 | async-start | bytes 8912896 | tf_op jit(solution)/shard_map/all_gather | solution.py:241
  612.7 252.0 %reduce-scatter.11.cloned.1.call-start = ((), (), s32[]{:S(2)}) async-start(), calls=%async_computation.10 | async-start | bytes 8912896 | tf_op jit(solution)/shard_map/reduce_scatter | solution.py:267
  746.1 181.5 %reduce-scatter.9.cloned.1.call-start = ((), (), s32[]{:S(2)}) async-start(), calls=%async_computation.9 | async-start | bytes 8912896 | tf_op jit(solution)/shard_map/reduce_scatter | solution.py:244
  768.0 26.4 %collective-permute-start.31 = (bf16[512,4,256]{2,0,1:T(8,128)(2,1)}, bf16[512,4,256]{2,0,1:T(8,128)(2,1)}, u32[]{:S(2)}, u32[]{:S(2)}) collective-permute-start(bf16[512,4,256]{2,0,1:T(8,128)(2,1)} %select_convert_fusion), channel_id=1, source_target_pairs={{0,64},{32,96},{64,0},{96,32},{1,65},{33,97},{65,1},{97,33},{2,66}... | collective-permute-start | bytes 3145736 | tf_op jit(solution)/shard_map/ppermute | solution.py:360
  779.4 36.3 %collective-permute-start.28 = (bf16[4,256,512]{2,1,0:T(8,128)(2,1)}, bf16[4,256,512]{2,1,0:T(8,128)(2,1)}, u32[]{:S(2)}, u32[]{:S(2)}) collective-permute-start(bf16[4,256,512]{2,1,0:T(8,128)(2,1)} %bitcast.57), channel_id=1, source_target_pairs={{0,64},{32,96},{64,0},{96,32},{1,65},{33,97},{65,1},{97,33},{2,66}... | collective-permute-start | bytes 3145736 | tf_op jit(solution)/shard_map/ppermute | solution.py:360
  796.5 21.1 %collective-permute-start.32 = (bf16[512,2,256]{2,0,1:T(8,128)(2,1)S(1)}, bf16[512,2,256]{2,0,1:T(8,128)(2,1)S(1)}, u32[]{:S(2)}, u32[]{:S(2)}) collective-permute-start(bf16[512,2,256]{2,0,1:T(8,128)(2,1)S(1)} %select_convert_fusion.3), channel_id=1, source_target_pairs={{0,32},{32,0},{64,96},{96,64},{1,33},{33,1},{65,97},{97,65},{2,34}... | collective-permute-start | bytes 1572872 | tf_op jit(solution)/shard_map/ppermute | solution.py:360
  817.5 4.4 collective-permute-start.29
  818.6 10.9 %collective-permute-start.33 = (bf16[512,1,256]{2,0,1:T(8,128)(2,1)}, bf16[512,1,256]{2,0,1:T(8,128)(2,1)S(1)}, u32[]{:S(2)}, u32[]{:S(2)}) collective-permute-start(bf16[512,1,256]{2,0,1:T(8,128)(2,1)} %select_convert_fusion.5), channel_id=1, source_target_pairs={{0,16},{16,0},{1,17},{17,1},{2,18},{18,2},{3,19},{19,3},{4,20},{20... | collective-permute-start | bytes 786440 | tf_op jit(solution)/shard_map/ppermute | solution.py:360
  823.2 11.5 %collective-permute-start.30 = (bf16[1,256,512]{2,1,0:T(8,128)(2,1)S(1)}, bf16[1,256,512]{2,1,0:T(8,128)(2,1)S(1)}, u32[]{:S(2)}, u32[]{:S(2)}) collective-permute-start(bf16[1,256,512]{2,1,0:T(8,128)(2,1)S(1)} %select_convert_fusion.6), channel_id=1, source_target_pairs={{0,16},{16,0},{1,17},{17,1},{2,18},{18,2},{3,19},{19,3},{4,20},{20... | collective-permute-start | bytes 786440 | tf_op jit(solution)/shard_map/ppermute | solution.py:360
  844.4 10.1 %collective-permute-start.25 = (bf16[1,128,4,256]{3,1,2,0:T(8,128)(2,1)S(1)}, bf16[1,128,4,256]{3,1,2,0:T(8,128)(2,1)S(1)}, u32[]{:S(2)}, u32[]{:S(2)}) collective-permute-start(bf16[1,128,4,256]{3,1,2,0:T(8,128)(2,1)S(1)} %select_convert_fusion.7), channel_id=1, source_target_pairs={{0,64},{32,96},{64,0},{96,32},{1,65},{33,97},{65,1},{97,33},{2,66}... | collective-permute-start | bytes 786440 | tf_op jit(solution)/shard_map/ppermute | solution.py:360
  854.8 1.6 collective-permute-start.26
  857.1 6.1 collective-permute-start.27
  862.6 36.4 %collective-permute-start.22 = (bf16[4,256,3,1,128]{4,3,2,1,0:T(2,128)(2,1)S(1)}, bf16[4,256,3,1,128]{4,3,2,1,0:T(2,128)(2,1)}, u32[]{:S(2)}, u32[]{:S(2)}) collective-permute-start(bf16[4,256,3,1,128]{4,3,2,1,0:T(2,128)(2,1)S(1)} %copy.55), channel_id=1, source_target_pairs={{0,64},{32,96},{64,0},{96,32},{1,65},{33,97},{65,1},{97,33},{2,66}... | collective-permute-start | bytes 2359304 | tf_op jit(solution)/shard_map/ppermute | solution.py:360
  869.2 34.2 %collective-permute-start.15 = (f32[8,8,192]{2,0,1:T(8,128)S(1)}, f32[8,8,192]{2,0,1:T(8,128)S(1)}, u32[]{:S(2)}, u32[]{:S(2)}) collective-permute-start(f32[8,8,192]{2,0,1:T(8,128)S(1)} %slice_select_fusion.2), channel_id=1, source_target_pairs={{0,8},{1,9},{2,10},{3,11},{4,12},{5,13},{6,14},{7,15},{8,0},{9,1},... | collective-permute-start | bytes 147464 | tf_op jit(solution)/shard_map/ppermute | solution.py:360
  903.4 4.3 collective-permute-start.16
  905.8 5.1 collective-permute-start.23
  907.8 5.5 collective-permute-start.17
  913.3 3.8 collective-permute-start.18
  915.3 9.4 collective-permute-start.24
  917.1 9.0 collective-permute-start.19
  926.1 1.2 collective-permute-start.20
  927.4 5.2 collective-permute-start.21
  (115 other events, 1363.5 us)
Sparse Core Ops, SparseCore 0:
  12.4 73.0 all-gather.3
  87.6 70.3 all-gather.5
  161.4 84.6 reduce-scatter.4
  525.6 81.1 reduce-scatter.6
  612.9 70.0 all-gather.7
  746.2 84.7 reduce-scatter.10
  834.5 85.3 reduce-scatter.8
